TPU v7x, 256 devices: a whole 4x4x8 slice. The times are simulated.
256 devices in a mesh: pipe: 4 (over x), expert: 16 (over z, core), dp: 4 (over y).
Axes of the slice: x: 4, y: 4, z: 8, core: 2. Of those that a mesh axis runs over, the one named last changes fastest.
Arguments:
- tokens: bfloat16 [4, 8192, 2048], P('pipe', ('expert', 'dp')), may hold values from -6 to 6
- cotangent: bfloat16 [4, 8192, 2048], P('pipe', ('expert', 'dp')), may hold values from -6 to 6
- norm_gain: float32 [4, 2048], P('pipe'), may hold values from 0.5 to 1.5
- first_ids: int32 [4, 8192, 2], P('pipe', ('expert', 'dp')), may hold values from 0 to 7, all different within a row; in each aligned block of 128 rows (0 to 127, 128 to 255, ..., all dimensions but the last counted through in order) at most 36 rows name the same one
- first_gates: float32 [4, 8192, 2], P('pipe', ('expert', 'dp')), may hold values from 0.1 to 1
- second_ids: int32 [4, 8192, 2], P('pipe', ('expert', 'dp')), may hold values from 0 to 7, all different within a row; in each aligned block of 128 rows (0 to 127, 128 to 255, ..., all dimensions but the last counted through in order) at most 36 rows name the same one
- second_gates: float32 [4, 8192, 2], P('pipe', ('expert', 'dp')), may hold values from 0.1 to 1
- new_slot: int32 [4, 8], P('pipe'), may hold values from 0 to 7, each once within a row
- inner_weight: float32 [4, 16, 2, 2048, 384], P('pipe', 'expert', None, 'dp'), may hold values from -0.125 to 0.125
- outer_weight: float32 [4, 16, 384, 2048], P('pipe', 'expert', None, 'dp'), may hold values from -0.21875 to 0.21875
- inner_mean: bfloat16 [4, 16, 2, 2048, 384], P('pipe', 'expert', None, 'dp'), may hold values from -60 to 60
- outer_mean: bfloat16 [4, 16, 384, 2048], P('pipe', 'expert', None, 'dp'), may hold values from -60 to 60
- inner_square: bfloat16 [4, 16, 2, 2048, 384], P('pipe', 'expert', None, 'dp'), may hold values from 10 to 1000
- outer_square: bfloat16 [4, 16, 384, 2048], P('pipe', 'expert', None, 'dp'), may hold values from 10 to 1000
Outputs:
- layer_out: bfloat16 [4, 8192, 2048], P('pipe', ('expert', 'dp'))
- weight_inner: float32 [4, 16, 2, 2048, 384], P('pipe', 'expert', None, 'dp')
- weight_outer: float32 [4, 16, 384, 2048], P('pipe', 'expert', None, 'dp')
- mean_inner: bfloat16 [4, 16, 2, 2048, 384], P('pipe', 'expert', None, 'dp')
- mean_outer: bfloat16 [4, 16, 384, 2048], P('pipe', 'expert', None, 'dp')
- square_inner: bfloat16 [4, 16, 2, 2048, 384], P('pipe', 'expert', None, 'dp')
- square_outer: bfloat16 [4, 16, 384, 2048], P('pipe', 'expert', None, 'dp')
Inputs may be any that keep to these rules, and one draw needn't show every extreme that they name: `first_ids`: each token names 2 different experts. Within the rows of one device no expert is named more than 36 times, and some device names some expert exactly 36 times. `second_ids`: as first_ids. `new_slot`: for each section, a permutation of the 8 experts.
All inputs are finite; a program needn't handle non-finite values.
Results may differ from a plain program's by a relative error of at most 0.008.
Values may be sent and summed in bfloat16 or wider, within the bound.
No kernel may reach another device: no remote copies, remote signals or barrier semaphores. Data moves between devices by JAX's collectives and lax.ppermute only.
A program may use at most 128 MiB of HBM per device.

v0:
```python
import jax
import jax.numpy as jnp
from jax import lax
from jax.sharding import PartitionSpec as P

norm_eps = 1e-06
learn_rate = 0.001
beta_one = 0.9
beta_two = 0.95
adam_eps = 1e-08
bias_one = 0.999973438601112
bias_two = 0.994079470779667


def side_by_side(arrays, axis, split_dim, concat_dim, along):
    ends, at = ([], 0)
    for a in arrays[:-1]:
        at += a.shape[along]
        ends.append(at)
    both = jnp.concatenate(arrays, axis=along)
    return tuple(
        jnp.split(
            lax.all_to_all(both, axis, split_axis=split_dim, concat_axis=concat_dim, tiled=True),
            ends,
            axis=along,
        )
    )


def for_sending(array):

    def short(part):
        return part.astype(jnp.bfloat16) if part.dtype == jnp.float32 else part

    return jax.tree.map(short, array)


def cut_along(array, dim, size):
    before, after = (array.shape[:dim], array.shape[dim + 1 :])
    return jnp.moveaxis(array.reshape(*before, size, -1, *after), dim, 0)


def sum_together(arrays, axis, dims):
    size = lax.axis_size(axis)
    parts = [cut_along(a, dim, size) for a, dim in zip(arrays, dims)]
    lines = jnp.concatenate([b.reshape(size, -1) for b in parts], axis=1)
    rows = max(16, -(-lines.shape[1] // 1024) * 8)
    lines = jnp.pad(lines, ((0, 0), (0, rows * 128 - lines.shape[1]))).reshape(-1, 128)
    line, at, outs = (lax.psum_scatter(lines, axis, tiled=True).reshape(-1), 0, [])
    for b in parts:
        part = b[0]
        outs.append(line[at : at + part.size].reshape(part.shape))
        at += part.size
    return tuple(outs)


def passed_along(block, axis, distance):
    devices = range(lax.axis_size(axis))
    route = [((i - distance) % len(devices), i) for i in devices]
    return lax.ppermute(block, axis, route)


def normed(values, gain_row):
    widened = values.astype(jnp.float32)
    inverse_rms = lax.rsqrt(jnp.mean(widened * widened, axis=-1, keepdims=True) + norm_eps)
    return (widened * inverse_rms * gain_row).astype(jnp.bfloat16)


def silu_parts(gate_proj):
    logistic = jax.nn.sigmoid(gate_proj)
    return (gate_proj * logistic, logistic * (1.0 + gate_proj * (1.0 - logistic)))


def half_forward(token_rows, inner_full, outer_full):
    gate_proj = jnp.dot(token_rows, inner_full[0], preferred_element_type=jnp.float32)
    up_proj = jnp.dot(token_rows, inner_full[1], preferred_element_type=jnp.float32)
    activity = (silu_parts(gate_proj)[0] * up_proj).astype(jnp.bfloat16)
    half_out = jnp.dot(activity, outer_full, preferred_element_type=jnp.float32).astype(
        jnp.bfloat16
    )
    return (half_out, activity, gate_proj, up_proj)


def half_backward(token_rows, grad_rows, outer_full, activity, gate_proj, up_proj):
    grad_outer = jnp.dot(activity.T, grad_rows, preferred_element_type=jnp.float32)
    d_active = jnp.dot(grad_rows, outer_full.T, preferred_element_type=jnp.float32)
    swish_value, swish_slope = silu_parts(gate_proj)
    d_gate = (d_active * up_proj * swish_slope).astype(jnp.bfloat16)
    d_upper = (d_active * swish_value).astype(jnp.bfloat16)
    grad_gate = jnp.dot(token_rows.T, d_gate, preferred_element_type=jnp.float32)
    grad_upper = jnp.dot(token_rows.T, d_upper, preferred_element_type=jnp.float32)
    return (jnp.stack([grad_gate, grad_upper]), grad_outer)


def slot_index(ids, pair_of, capacity):
    flattened = ids.reshape(-1)
    expert_row = jnp.arange(pair_of.shape[0], dtype=jnp.int32)
    onehot = (flattened[:, None] == expert_row[None, :]).astype(jnp.int32)
    ranking = jnp.sum((jnp.cumsum(onehot, axis=0) - 1) * onehot, axis=1)
    target = jnp.sum(onehot * pair_of[None, :], axis=1)
    return (target * capacity + ranking).reshape(ids.shape)


def selection(slots, values, total_slots):
    positions = jnp.arange(total_slots, dtype=jnp.int32)
    result = jnp.zeros((total_slots, slots.shape[0]), jnp.float32)
    for column in range(slots.shape[1]):
        result = result + jnp.where(
            slots[:, column][None, :] == positions[:, None], values[:, column][None, :], 0.0
        )
    return result


def both_halves(packed, pair_count, capacity):
    return jnp.repeat(packed.reshape(pair_count, capacity, packed.shape[-1]), 2, axis=0)


def gather_weights(inner_master, outer_master):
    inner_full, outer_full = (
        lax.all_gather(inner_master.astype(jnp.bfloat16), "dp", axis=3, tiled=True),
        lax.all_gather(outer_master.astype(jnp.bfloat16), "dp", axis=3, tiled=True),
    )
    return (inner_full[0, 0], outer_full[0, 0])


def forward_layer(token_rows, gain_row, ids, gates, pair_of, inner_full, outer_full, capacity):
    pair_count = pair_of.shape[0]
    normal = normed(token_rows, gain_row)
    slots = slot_index(ids, pair_of, capacity)
    picker = selection(slots, jnp.ones(slots.shape, jnp.float32), pair_count * capacity).astype(
        jnp.bfloat16
    )
    packed = jnp.dot(picker, normal, preferred_element_type=jnp.float32).astype(jnp.bfloat16)
    send_rows = both_halves(packed, pair_count, capacity)
    arrived = lax.all_to_all(send_rows, "expert", split_axis=0, concat_axis=0, tiled=True)
    shape = arrived.shape
    half_out, activity, gate_proj, up_proj = half_forward(
        arrived.reshape(-1, shape[-1]), inner_full, outer_full
    )
    hidden = activity.shape[-1]
    half_out, arrived, activity, gate_proj, up_proj = (
        half_out.reshape(shape),
        arrived,
        activity.reshape(shape[0], shape[1], hidden),
        gate_proj.reshape(shape[0], shape[1], hidden),
        up_proj.reshape(shape[0], shape[1], hidden),
    )
    returned = lax.all_to_all(half_out, "expert", split_axis=0, concat_axis=0, tiled=True)
    summed = returned.astype(jnp.float32).reshape(pair_count, 2, capacity, -1).sum(axis=1)
    summed = summed.reshape(pair_count * capacity, -1)
    picked = summed[slots]
    mixed_rows = token_rows.astype(jnp.float32) + jnp.sum(gates[..., None] * picked, axis=1)
    return (mixed_rows.astype(jnp.bfloat16), (slots, arrived, activity, gate_proj, up_proj))


def adam_step(weight, mean, square, grads):
    mean_new = (beta_one * mean.astype(jnp.float32) + (1.0 - beta_one) * grads).astype(jnp.bfloat16)
    square_new = (beta_two * square.astype(jnp.float32) + (1.0 - beta_two) * grads * grads).astype(
        jnp.bfloat16
    )
    mean_wide = lax.optimization_barrier(mean_new).astype(jnp.float32)
    square_wide = lax.optimization_barrier(square_new).astype(jnp.float32)
    update = mean_wide / bias_one / (jnp.sqrt(square_wide / bias_two) + adam_eps)
    return (weight - learn_rate * update, mean_new, square_new)


def relocate_master(inner_master, outer_master, source):
    devices = source.shape[0]
    inner_spread, outer_spread = tuple(
        (
            part.astype(jnp.float32)
            for part in side_by_side(
                (
                    inner_master.reshape(devices, -1).astype(jnp.bfloat16),
                    outer_master.reshape(devices, -1).astype(jnp.bfloat16),
                ),
                "expert",
                0,
                0,
                1,
            )
        )
    )
    inner_order = jnp.take(inner_spread, source, axis=0)
    outer_order = jnp.take(outer_spread, source, axis=0)
    inner_back, outer_back = (
        lax.all_to_all(
            for_sending(inner_order), "expert", split_axis=0, concat_axis=0, tiled=True
        ).astype(inner_order.dtype),
        lax.all_to_all(
            for_sending(outer_order), "expert", split_axis=0, concat_axis=0, tiled=True
        ).astype(outer_order.dtype),
    )
    return (inner_back.reshape(inner_master.shape), outer_back.reshape(outer_master.shape))


def relocate_moments(first_inner, first_outer, second_inner, second_outer, source):
    devices = source.shape[0]
    spread = side_by_side(
        (
            first_inner.reshape(devices, -1),
            first_outer.reshape(devices, -1),
            second_inner.reshape(devices, -1),
            second_outer.reshape(devices, -1),
        ),
        "expert",
        0,
        0,
        1,
    )
    ordered = [jnp.take(member, source, axis=0) for member in spread]
    back = side_by_side((ordered[0], ordered[1], ordered[2], ordered[3]), "expert", 0, 0, 1)
    return (
        back[0].reshape(first_inner.shape),
        back[1].reshape(first_outer.shape),
        back[2].reshape(second_inner.shape),
        back[3].reshape(second_outer.shape),
    )


def per_device(
    tokens,
    cotangent,
    norm_gain,
    first_ids,
    first_gates,
    second_ids,
    second_gates,
    new_slot,
    inner_weight,
    outer_weight,
    inner_mean,
    outer_mean,
    inner_square,
    outer_square,
):
    pair_count = new_slot.shape[1]
    rows_here = tokens.shape[1]
    top_count = first_ids.shape[2]
    width = tokens.shape[2]
    usual = rows_here * top_count // pair_count
    capacity = min(rows_here, usual + usual // 8)
    gain_row = norm_gain[0]
    identity_map = jnp.arange(pair_count, dtype=jnp.int32)
    inner_full, outer_full = gather_weights(inner_weight, outer_weight)
    first_out, saved = forward_layer(
        tokens[0],
        gain_row,
        first_ids[0],
        first_gates[0],
        identity_map,
        inner_full,
        outer_full,
        capacity,
    )
    slots, arrived, activity, gate_proj, up_proj = saved
    weighting = selection(slots, first_gates[0], pair_count * capacity)
    grad_packed = jnp.dot(
        weighting, cotangent[0].astype(jnp.float32), precision=lax.Precision.HIGHEST
    ).astype(jnp.bfloat16)
    grad_send = both_halves(grad_packed, pair_count, capacity)
    grad_arrived = lax.all_to_all(grad_send, "expert", split_axis=0, concat_axis=0, tiled=True)
    hidden = activity.shape[-1]
    grad_inner, grad_outer = half_backward(
        arrived.reshape(-1, width),
        grad_arrived.reshape(-1, width),
        outer_full,
        activity.reshape(-1, hidden),
        gate_proj.reshape(-1, hidden),
        up_proj.reshape(-1, hidden),
    )
    sum_inner, sum_outer = tuple(
        (
            part.astype(jnp.float32)
            for part in sum_together(
                (
                    grad_inner[None, None].astype(jnp.bfloat16),
                    grad_outer[None, None].astype(jnp.bfloat16),
                ),
                "dp",
                (3, 3),
            )
        )
    )
    stepped_inner, mean_in_new, square_in_new = adam_step(
        inner_weight, inner_mean, inner_square, sum_inner
    )
    stepped_outer, mean_out_new, square_out_new = adam_step(
        outer_weight, outer_mean, outer_square, sum_outer
    )
    new_pairs = new_slot[0]
    inverse = jnp.sum(
        jnp.where(new_pairs[:, None] == identity_map[None, :], identity_map[:, None], 0), axis=0
    )
    device_ids = jnp.arange(2 * pair_count, dtype=jnp.int32)
    source = 2 * jnp.repeat(inverse, 2) + device_ids % 2
    moved_inner, moved_outer = relocate_master(stepped_inner, stepped_outer, source)
    moved_mean_in, moved_mean_out, moved_square_in, moved_square_out = relocate_moments(
        mean_in_new, mean_out_new, square_in_new, square_out_new, source
    )
    inner_two, outer_two = gather_weights(moved_inner, moved_outer)
    shifted = passed_along(first_out, "pipe", 1)
    second_out, unused = forward_layer(
        shifted, gain_row, second_ids[0], second_gates[0], new_pairs, inner_two, outer_two, capacity
    )
    return (
        second_out[None],
        moved_inner,
        moved_outer,
        moved_mean_in,
        moved_mean_out,
        moved_square_in,
        moved_square_out,
    )


def solution(mesh):
    return jax.shard_map(
        per_device,
        mesh=mesh,
        in_specs=(
            P("pipe", ("expert", "dp"), None),
            P("pipe", ("expert", "dp"), None),
            P("pipe", None),
            P("pipe", ("expert", "dp"), None),
            P("pipe", ("expert", "dp"), None),
            P("pipe", ("expert", "dp"), None),
            P("pipe", ("expert", "dp"), None),
            P("pipe", None),
            P("pipe", "expert", None, "dp", None),
            P("pipe", "expert", None, "dp"),
            P("pipe", "expert", None, "dp", None),
            P("pipe", "expert", None, "dp"),
            P("pipe", "expert", None, "dp", None),
            P("pipe", "expert", None, "dp"),
        ),
        out_specs=(
            P("pipe", ("expert", "dp"), None),
            P("pipe", "expert", None, "dp", None),
            P("pipe", "expert", None, "dp"),
            P("pipe", "expert", None, "dp", None),
            P("pipe", "expert", None, "dp"),
            P("pipe", "expert", None, "dp", None),
            P("pipe", "expert", None, "dp"),
        ),
        check_vma=False,
    )
```

profile of v0, /device:TPU:1, one launch (start us, length us, event | category | flops | bytes accessed | tf_op | source)
XLA Modules:
  0.0 659.8 jit_solution(6963974720981108128)
XLA Ops:
  14.6 10.1 %all-to-all-start = ((bf16[16,36,2048]{2,1,0:T(8,128)(2,1)}), bf16[16,36,2048]{2,1,0:T(8,128)(2,1)S(1)}, u32[]{:S(2)}, u32[]{:S(2)}) async-start(bf16[16,36,2048]{2,1,0:T(8,128)(2,1)} %bitcast.153), calls=%async_computation | async-start | bytes 5242880 | tf_op jit(solution)/shard_map/all_to_all | solution.py:135
  31.1 53.4 %all-to-all-done = bf16[16,36,2048]{2,1,0:T(8,128)(2,1)S(1)} async-done(((bf16[16,36,2048]{2,1,0:T(8,128)(2,1)}), bf16[16,36,2048]{2,1,0:T(8,128)(2,1)S(1)}, u32[]{:S(2)}, u32[]{:S(2)}) %all-to-all-start) | async-done | bytes 2359328 | tf_op jit(solution)/shard_map/all_to_all | solution.py:135
  87.6 5.4 all-to-all-start.3
  98.2 54.7 %all-to-all-done.3 = bf16[16,36,2048]{2,1,0:T(8,128)(2,1)} async-done(((bf16[16,36,2048]{2,1,0:T(8,128)(2,1)}), bf16[16,36,2048]{2,1,0:T(8,128)(2,1)}, u32[]{:S(2)}, u32[]{:S(2)}) %all-to-all-start.3) | async-done | bytes 2359328 | tf_op jit(solution)/shard_map/all_to_all | solution.py:262
  170.5 4.7 reshape.547
  180.7 20.7 %pad_maximum_fusion = bf16[4,589824]{1,0:T(4,128)(2,1)} fusion(bf16[4,196608]{1,0:T(4,128)(2,1)S(1)} %bitcast.159, bf16[4,393216]{1,0:T(4,128)(2,1)} %reshape.547), kind=kLoop, calls=%fused_computation.10 | loop fusion | flops 9437184 | bytes 9437184 | tf_op jit(solution)/shard_map/concatenate | solution.py:46
  201.4 9.2 %reshape.550 = bf16[18432,128]{1,0:T(8,128)(2,1)} reshape(bf16[4,589824]{1,0:T(4,128)(2,1)} %pad_maximum_fusion) | data formatting | bytes 9437184 | tf_op jit(solution)/shard_map/reshape | solution.py:48
  215.6 5.4 all-to-all-start.1
  221.0 42.7 %reduce-scatter.2.cloned.1.call-done = bf16[4608,128]{1,0:T(8,128)(2,1)} async-done(((bf16[18432,128]{1,0:T(8,128)(2,1)}), bf16[4608,128]{1,0:T(8,128)(2,1)}) %reduce-scatter.2.cloned.1.call-update) | async-done | bytes 1179664 | tf_op jit(solution)/shard_map/reduce_scatter | solution.py:49
  293.9 8.2 %all-to-all-start.4 = ((bf16[16,2,18432]{2,1,0:T(2,128)(2,1)}), bf16[16,2,18432]{2,1,0:T(2,128)(2,1)}, u32[]{:S(2)}, u32[]{:S(2)}) async-start(bf16[16,2,18432]{2,1,0:T(2,128)(2,1)} %reshape.658), calls=%async_computation.5 | async-start | bytes 2359296 | tf_op jit(solution)/shard_map/all_to_all | solution.py:23
  321.5 11.1 %all-to-all-done.4 = bf16[16,2,18432]{2,1,0:T(2,128)(2,1)} async-done(((bf16[16,2,18432]{2,1,0:T(2,128)(2,1)}), bf16[16,2,18432]{2,1,0:T(2,128)(2,1)}, u32[]{:S(2)}, u32[]{:S(2)}) %all-to-all-start.4) | async-done | bytes 1179680 | tf_op jit(solution)/shard_map/all_to_all | solution.py:23
  332.6 4.4 reshape.659
  356.5 13.4 %all-to-all-done.5 = bf16[16,2,12288]{2,1,0:T(2,128)(2,1)} async-done(((bf16[16,2,12288]{2,1,0:T(2,128)(2,1)}), bf16[16,2,12288]{2,1,0:T(2,128)(2,1)}, u32[]{:S(2)}, u32[]{:S(2)}) %all-to-all-start.5) | async-done | bytes 786464 | tf_op jit(solution)/shard_map/all_to_all | solution.py:187
  373.8 4.8 multiply_reduce_fusion.1
  380.5 13.4 %collective-permute-done = bf16[128,2048]{1,0:T(8,128)(2,1)S(1)} collective-permute-done((bf16[128,2048]{1,0:T(8,128)(2,1)S(1)}, bf16[128,2048]{1,0:T(8,128)(2,1)S(1)}, u32[]{:S(2)}, u32[]{:S(2)}) %collective-permute-start) | collective-permute-done | bytes 524320 | tf_op jit(solution)/shard_map/ppermute | solution.py:60
  403.6 5.2 reshape.663
  408.8 6.9 %reduce.6 = bf16[16,24576]{1,0:T(8,128)(2,1)} reduce(bf16[16,1,24576]{2,1,0:T(2,128)(2,1)} %reshape.663, bf16[]{:T(256)} %constant.144), dimensions={1}, to_apply=%all_to_all.58.reduce_sub_computation | reduce | bytes 1572866 | tf_op jit(solution)/shard_map/all_to_all | solution.py:187
  418.1 9.3 %all-to-all-done.8 = bf16[16,2,36864]{2,1,0:T(2,128)(2,1)S(1)} async-done(((bf16[16,2,36864]{2,1,0:T(2,128)(2,1)}), bf16[16,2,36864]{2,1,0:T(2,128)(2,1)S(1)}, u32[]{:S(2)}, u32[]{:S(2)}) %all-to-all-start.8) | async-done | bytes 2359328 | tf_op jit(solution)/shard_map/all_to_all | solution.py:23
  430.7 5.5 all-to-all-start.2
  436.2 7.0 %reshape.665 = bf16[16,1,73728]{2,1,0:T(2,128)(2,1)} reshape(bf16[16,2,36864]{2,1,0:T(2,128)(2,1)S(1)} %all-to-all-done.8) | data formatting | bytes 4718592
  443.2 5.0 copy.105
  454.3 41.7 %all-to-all-done.2 = bf16[16,36,2048]{2,1,0:T(8,128)(2,1)} async-done(((bf16[16,36,2048]{2,1,0:T(8,128)(2,1)}), bf16[16,36,2048]{2,1,0:T(8,128)(2,1)}, u32[]{:S(2)}, u32[]{:S(2)}) %all-to-all-start.2) | async-done | bytes 2359328 | tf_op jit(solution)/shard_map/all_to_all | solution.py:135
  495.9 5.4 all-to-all-start.6
  510.3 5.6 all-to-all-done.6
  534.0 4.5 fusion.15
  538.6 14.7 %all-gather.11.cloned.1.call-done = bf16[1,1,384,2048]{3,2,1,0:T(8,128)(2,1)} async-done(((bf16[1,1,384,512]{3,2,1,0:T(8,128)(2,1)}), bf16[1,1,384,2048]{3,2,1,0:T(8,128)(2,1)}) %all-gather.11.cloned.1.call-update) | async-done | bytes 1572880 | tf_op jit(solution)/shard_map/all_gather | solution.py:121
  553.2 6.9 %convolution_convert_fusion = bf16[576,2048]{1,0:T(8,128)(2,1)} fusion(bf16[1,1,384,2048]{3,2,1,0:T(8,128)(2,1)} %all-gather.11.cloned.1.call-done, bf16[576,2048]{1,0:T(8,128)(2,1)} %reshape.542, bf16[1,1,2,2048,384]{4,3,2,1,0:T(8,128)(2,1)} %all-gather.9.cloned.1.call-done, f32[576,384]{1,0:T(8,128)} %fusion.15), kind=kOutput, calls=%fused_computation.12 | convolution fusion | flops 1814446080 | bytes 8749056 | tf_op jit(solution)/shard_map/dot_general | solution.py:78
  564.3 8.8 %all-to-all-done.9 = bf16[16,2,36864]{2,1,0:T(2,128)(2,1)S(1)} async-done(((bf16[16,2,36864]{2,1,0:T(2,128)(2,1)}), bf16[16,2,36864]{2,1,0:T(2,128)(2,1)S(1)}, u32[]{:S(2)}, u32[]{:S(2)}) %all-to-all-start.9) | async-done | bytes 2359328 | tf_op jit(solution)/shard_map/all_to_all | solution.py:23
  574.5 5.5 all-to-all-start.7
  580.0 10.7 %reshape.667 = bf16[16,1,73728]{2,1,0:T(2,128)(2,1)} reshape(bf16[16,2,36864]{2,1,0:T(2,128)(2,1)} %copy-done.2) | data formatting | bytes 4718592
  590.7 4.9 copy.104
  606.1 33.7 %all-to-all-done.7 = bf16[16,36,2048]{2,1,0:T(8,128)(2,1)S(1)} async-done(((bf16[16,36,2048]{2,1,0:T(8,128)(2,1)}), bf16[16,36,2048]{2,1,0:T(8,128)(2,1)S(1)}, u32[]{:S(2)}, u32[]{:S(2)}) %all-to-all-start.7) | async-done | bytes 2359328 | tf_op jit(solution)/shard_map/all_to_all | solution.py:148
  (223 shorter events, 202.3 us)
Async XLA Ops:
  7.2 19.5 %copy-start = (bf16[1,128,2048]{2,1,0:T(8,128)(2,1)S(1)}, bf16[1,128,2048]{2,1,0:T(8,128)(2,1)}, u32[]{:S(2)}) copy-start(bf16[1,128,2048]{2,1,0:T(8,128)(2,1)} %param.19) | copy-start | bytes 1572868
  14.6 12.1 %copy-start.24 = (f32[1,128,2]{1,2,0:T(2,128)S(1)}, f32[1,128,2]{1,2,0:T(2,128)}, u32[]{:S(2)}) copy-start(f32[1,128,2]{1,2,0:T(2,128)} %param.22) | copy-start | bytes 3076
  14.6 69.9 %all-to-all-start = ((bf16[16,36,2048]{2,1,0:T(8,128)(2,1)}), bf16[16,36,2048]{2,1,0:T(8,128)(2,1)S(1)}, u32[]{:S(2)}, u32[]{:S(2)}) async-start(bf16[16,36,2048]{2,1,0:T(8,128)(2,1)} %bitcast.153), calls=%async_computation | async-start | bytes 5242880 | tf_op jit(solution)/shard_map/all_to_all | solution.py:135
  24.7 130.9 %all-gather.7.cloned.1.call-start = ((), (), s32[]{:S(2)}) async-start(), calls=%async_computation.12 | async-start | bytes 1966080 | tf_op jit(solution)/shard_map/all_gather | solution.py:121
  87.6 65.3 %all-to-all-start.3 = ((bf16[16,36,2048]{2,1,0:T(8,128)(2,1)}), bf16[16,36,2048]{2,1,0:T(8,128)(2,1)}, u32[]{:S(2)}, u32[]{:S(2)}) async-start(bf16[16,36,2048]{2,1,0:T(8,128)(2,1)} %bitcast.154), calls=%async_computation.3 | async-start | bytes 5242880 | tf_op jit(solution)/shard_map/all_to_all | solution.py:262
  93.0 66.3 %all-gather.5.cloned.1.call-start = ((), (), s32[]{:S(2)}) async-start(), calls=%async_computation.11 | async-start | bytes 3932160 | tf_op jit(solution)/shard_map/all_gather | solution.py:120
  95.5 168.2 %reduce-scatter.2.cloned.1.call-start = ((), (), s32[]{:S(2)}) async-start(), calls=%async_computation.13 | async-start | bytes 5898240 | tf_op jit(solution)/shard_map/reduce_scatter | solution.py:49
  215.6 78.3 %all-to-all-start.1 = ((bf16[16,36,2048]{2,1,0:T(8,128)(2,1)}), bf16[16,36,2048]{2,1,0:T(8,128)(2,1)S(1)}, u32[]{:S(2)}, u32[]{:S(2)}) async-start(bf16[16,36,2048]{2,1,0:T(8,128)(2,1)} %reshape.535), calls=%async_computation.1 | async-start | bytes 5242880 | tf_op jit(solution)/shard_map/all_to_all | solution.py:148
  291.1 11.0 %copy-start.27 = (s32[1,8]{1,0:T(1,128)S(1)}, s32[1,8]{1,0:T(1,128)}, u32[]{:S(2)}) copy-start(s32[1,8]{1,0:T(1,128)} %param.25) | copy-start | bytes 100
  291.1 12.8 %copy-start.25 = (s32[1,128,2]{1,2,0:T(2,128)S(1)}, s32[1,128,2]{1,2,0:T(2,128)}, u32[]{:S(2)}) copy-start(s32[1,128,2]{1,2,0:T(2,128)} %param.23) | copy-start | bytes 3076
  293.9 38.7 %all-to-all-start.4 = ((bf16[16,2,18432]{2,1,0:T(2,128)(2,1)}), bf16[16,2,18432]{2,1,0:T(2,128)(2,1)}, u32[]{:S(2)}, u32[]{:S(2)}) async-start(bf16[16,2,18432]{2,1,0:T(2,128)(2,1)} %reshape.658), calls=%async_computation.5 | async-start | bytes 2359296 | tf_op jit(solution)/shard_map/all_to_all | solution.py:23
  314.3 4.8 copy-start.5
  340.7 6.9 %copy-start.16 = (bf16[16,12288]{1,0:T(8,128)(2,1)S(1)}, bf16[16,12288]{1,0:T(8,128)(2,1)}, u32[]{:S(2)}) copy-start(bf16[16,12288]{1,0:T(8,128)(2,1)} %reshape.556) | copy-start | bytes 1179652
  343.4 26.5 %all-to-all-start.5 = ((bf16[16,2,12288]{2,1,0:T(2,128)(2,1)}), bf16[16,2,12288]{2,1,0:T(2,128)(2,1)}, u32[]{:S(2)}, u32[]{:S(2)}) async-start(bf16[16,2,12288]{2,1,0:T(2,128)(2,1)} %reshape.662), calls=%async_computation.6 | async-start | bytes 1572864 | tf_op jit(solution)/shard_map/all_to_all | solution.py:187
  356.5 17.3 %copy-start.19 = (f32[128,2]{1,0:T(8,128)S(1)}, f32[128,2]{1,0:T(8,128)}, u32[]{:S(2)}) copy-start(f32[128,2]{1,0:T(8,128)} %copy.67) | copy-start | bytes 3076
  369.9 57.5 %all-to-all-start.8 = ((bf16[16,2,36864]{2,1,0:T(2,128)(2,1)}), bf16[16,2,36864]{2,1,0:T(2,128)(2,1)S(1)}, u32[]{:S(2)}, u32[]{:S(2)}) async-start(bf16[16,2,36864]{2,1,0:T(2,128)(2,1)} %reshape.664), calls=%async_computation.9 | async-start | bytes 4718592 | tf_op jit(solution)/shard_map/all_to_all | solution.py:23
  373.5 5.1 copy-start.10
  373.5 6.5 slice-start
  373.5 6.5 copy-start.23
  373.5 6.5 copy-start.28
  373.5 6.7 %copy-start.29 = (s32[16]{0:T(128)S(1)}, s32[16]{0:T(128)}, u32[]{:S(2)}) copy-start(s32[16]{0:T(128)} %get-tuple-element.18) | copy-start | bytes 196
  373.6 20.5 %copy-start.21 = (f32[1,2048]{1,0:T(1,128)S(1)}, f32[1,2048]{1,0:T(1,128)}, u32[]{:S(2)}) copy-start(f32[1,2048]{1,0:T(1,128)} %param.20) | copy-start | bytes 24580
  373.6 160.5 %all-gather.9.cloned.1.call-start = ((), (), s32[]{:S(2)}) async-start(), calls=%async_computation.14 | async-start | bytes 3932160 | tf_op jit(solution)/shard_map/all_gather | solution.py:120
  378.8 15.1 %collective-permute-start = (bf16[128,2048]{1,0:T(8,128)(2,1)S(1)}, bf16[128,2048]{1,0:T(8,128)(2,1)S(1)}, u32[]{:S(2)}, u32[]{:S(2)}) collective-permute-start(bf16[128,2048]{1,0:T(8,128)(2,1)S(1)} %fusion.38), channel_id=1, source_target_pairs={{192,0},{0,64},{64,128},{128,192},{193,1},{1,65},{65,129},{129,193... | collective-permute-start | bytes 1572872 | tf_op jit(solution)/shard_map/ppermute | solution.py:60
  430.7 65.3 %all-to-all-start.2 = ((bf16[16,36,2048]{2,1,0:T(8,128)(2,1)}), bf16[16,36,2048]{2,1,0:T(8,128)(2,1)}, u32[]{:S(2)}, u32[]{:S(2)}) async-start(bf16[16,36,2048]{2,1,0:T(8,128)(2,1)} %bitcast.15), calls=%async_computation.2 | async-start | bytes 5242880 | tf_op jit(solution)/shard_map/all_to_all | solution.py:135
  495.9 19.9 %all-to-all-start.6 = ((bf16[16,2,6144]{2,1,0:T(2,128)(2,1)}), bf16[16,2,6144]{2,1,0:T(2,128)(2,1)S(1)}, u32[]{:S(2)}, u32[]{:S(2)}) async-start(bf16[16,2,6144]{2,1,0:T(2,128)(2,1)} %reshape.660), calls=%async_computation.7 | async-start | bytes 786432 | tf_op jit(solution)/shard_map/all_to_all | solution.py:190
  515.9 57.1 %all-to-all-start.9 = ((bf16[16,2,36864]{2,1,0:T(2,128)(2,1)}), bf16[16,2,36864]{2,1,0:T(2,128)(2,1)S(1)}, u32[]{:S(2)}, u32[]{:S(2)}) async-start(bf16[16,2,36864]{2,1,0:T(2,128)(2,1)} %reshape.666), calls=%async_computation.10 | async-start | bytes 4718592 | tf_op jit(solution)/shard_map/all_to_all | solution.py:23
  519.5 6.3 copy-start.26
  519.5 33.7 %all-gather.11.cloned.1.call-start = ((), (), s32[]{:S(2)}) async-start(), calls=%async_computation.15 | async-start | bytes 1966080 | tf_op jit(solution)/shard_map/all_gather | solution.py:121
  526.5 4.1 copy-start.13
  574.5 65.2 %all-to-all-start.7 = ((bf16[16,36,2048]{2,1,0:T(8,128)(2,1)}), bf16[16,36,2048]{2,1,0:T(8,128)(2,1)S(1)}, u32[]{:S(2)}, u32[]{:S(2)}) async-start(bf16[16,36,2048]{2,1,0:T(8,128)(2,1)} %reshape.551), calls=%async_computation.8 | async-start | bytes 5242880 | tf_op jit(solution)/shard_map/all_to_all | solution.py:148
  646.4 6.7 %copy-start.1 = (bf16[1,128,2048]{2,1,0:T(8,128)(2,1)S(1)}, bf16[1,128,2048]{2,1,0:T(8,128)(2,1)}, u32[]{:S(2)}) copy-start(bf16[1,128,2048]{2,1,0:T(8,128)(2,1)} %param.19) | copy-start | bytes 1572868
  (17 other events, 39.5 us)
Sparse Core Ops, SparseCore 0:
  27.9 30.1 all-gather.6
  96.2 43.1 all-gather.4
  210.7 52.8 reduce-scatter.1
  418.2 39.8 all-gather.8
  525.6 27.5 all-gather.10
where the time goes:
time: 666 us; the launch traced here: 660 us
  waiting for transfers between devices  302 us (45%)
  local copies, waits for them, and re-layouts  160 us (24%)
  other arithmetic  88.4 us (13%)
  starting transfers between devices  59.5 us (9%)
  matrix products  34.5 us (5%)
  between operations  14.7 us (2%)
    all_to_all x2, waiting for transfers between devices, forward_layer(): lax.all_to_all(send_rows, 'expert', split_axis=0, concat_axis=0, tiled=True)  95.1 us
    unnamed x79, local copies, waits for them, and re-layouts  60 us
    all_to_all x1, waiting for transfers between devices, per_device(): lax.all_to_all(grad_send, 'expert', split_axis=0, concat_axis=0, tiled=True)  54.7 us
    reduce_scatter x1, waiting for transfers between devices, sum_together(): lax.psum_scatter(lines, axis, tiled=True).reshape(-1)  42.7 us
    all_to_all x2, waiting for transfers between devices, forward_layer(): lax.all_to_all(half_out, 'expert', split_axis=0, concat_axis=0, tiled=True)  33.7 us
    all_to_all x3, waiting for transfers between devices, side_by_side(): lax.all_to_all(both, axis, split_axis=split_dim, concat_axis=concat_dim,...  29.2 us
    concatenate x1, other arithmetic, sum_together(): lines = jnp.concatenate([b.reshape(size, -1) for b in parts], axis=1)  20.7 us
    all_to_all x2, starting transfers between devices, forward_layer(): lax.all_to_all(send_rows, 'expert', split_axis=0, concat_axis=0, tiled=True)  15.6 us
  transfers between devices with their start and end apart: 16, of which 12 were waited for; matrix products, arithmetic and copies ran while one was open for 29% of the time, Pallas kernels for 0%

commit v1 on v0

--- a/solution.py
+++ b/solution.py
@@ -118,7 +118,12 @@
 def gather_weights(inner_master, outer_master):
     inner_full, outer_full = (
         lax.all_gather(inner_master.astype(jnp.bfloat16), "dp", axis=3, tiled=True),
-        lax.all_gather(outer_master.astype(jnp.bfloat16), "dp", axis=3, tiled=True),
+        jnp.concatenate(
+            lax.all_to_all(
+                jnp.stack([outer_master.astype(jnp.bfloat16)] * lax.axis_size("dp")), "dp", 0, 0
+            ),
+            axis=3,
+        ),
     )
     return (inner_full[0, 0], outer_full[0, 0])
 

time: 666 us -> 763 us (1.15)
  waiting for transfers between devices: 302 us -> 395 us
  starting transfers between devices: 59.5 us -> 70.3 us
    all_to_all x2, waiting for transfers between devices: 33.7 us -> 79.2 us  [forward_layer(): lax.all_to_all(half_out, 'expert', split_axis=0, concat_axis=0, tiled=True)]
    all_to_all x0 -> x2, waiting for transfers between devices: none -> 25.9 us  [gather_weights(): lax.all_to_all(jnp.stack([outer_master.astype(jnp.bfloat16)] * lax.axis_s...]
    all_to_all x3, waiting for transfers between devices: 29.2 us -> 50.5 us  [side_by_side(): lax.all_to_all(both, axis, split_axis=split_dim, concat_axis=concat_dim,...]
    all_gather x2 -> x0, waiting for transfers between devices: 14.7 us -> none  [gather_weights(): lax.all_gather(outer_master.astype(jnp.bfloat16), 'dp', axis=3, tiled=True)]
    reduce_scatter x1, waiting for transfers between devices: 42.7 us -> 52.6 us  [sum_together(): lax.psum_scatter(lines, axis, tiled=True).reshape(-1)]
    all_to_all x0 -> x2, starting transfers between devices: none -> 8.71 us  [gather_weights(): lax.all_to_all(jnp.stack([outer_master.astype(jnp.bfloat16)] * lax.axis_s...]
  transfers between devices with their start and end apart: 16 -> 16, of which waited for: 12 -> 14; matrix products, arithmetic and copies ran while one was open for 29% -> 23% of each run, Pallas kernels for 0% -> 0%
where the time goes in v1:
time: 763 us; the launch traced here: 756 us
  waiting for transfers between devices  395 us (52%)
  local copies, waits for them, and re-layouts  159 us (21%)
  other arithmetic  81.4 us (11%)
  starting transfers between devices  70.3 us (9%)
  matrix products  34.9 us (5%)
  between operations  14.7 us (2%)
    all_to_all x2, waiting for transfers between devices, forward_layer(): lax.all_to_all(send_rows, 'expert', split_axis=0, concat_axis=0, tiled=True)  93.4 us
    all_to_all x2, waiting for transfers between devices, forward_layer(): lax.all_to_all(half_out, 'expert', split_axis=0, concat_axis=0, tiled=True)  79.2 us
    unnamed x79, local copies, waits for them, and re-layouts  62.1 us
    all_to_all x1, waiting for transfers between devices, per_device(): lax.all_to_all(grad_send, 'expert', split_axis=0, concat_axis=0, tiled=True)  56 us
    reduce_scatter x1, waiting for transfers between devices, sum_together(): lax.psum_scatter(lines, axis, tiled=True).reshape(-1)  52.6 us
    all_to_all x3, waiting for transfers between devices, side_by_side(): lax.all_to_all(both, axis, split_axis=split_dim, concat_axis=concat_dim,...  50.5 us
    all_to_all x2, waiting for transfers between devices, gather_weights(): lax.all_to_all(jnp.stack([outer_master.astype(jnp.bfloat16)] * lax.axis_s...  25.9 us
    concatenate x1, other arithmetic, sum_together(): lines = jnp.concatenate([b.reshape(size, -1) for b in parts], axis=1)  20.7 us
  transfers between devices with their start and end apart: 16, of which 14 were waited for; matrix products, arithmetic and copies ran while one was open for 23% of the time, Pallas kernels for 0%

profile of v1, /device:TPU:1, one launch (start us, length us, event | category | flops | bytes accessed | tf_op | source)
XLA Modules:
  0.0 755.9 jit_solution(11903421978836915751)
XLA Ops:
  14.6 10.1 %all-to-all-start = ((bf16[16,36,2048]{2,1,0:T(8,128)(2,1)}), bf16[16,36,2048]{2,1,0:T(8,128)(2,1)S(1)}, u32[]{:S(2)}, u32[]{:S(2)}) async-start(bf16[16,36,2048]{2,1,0:T(8,128)(2,1)} %bitcast.161), calls=%async_computation | async-start | bytes 5242880 | tf_op jit(solution)/shard_map/all_to_all | solution.py:140
  29.1 55.4 %all-to-all-done = bf16[16,36,2048]{2,1,0:T(8,128)(2,1)S(1)} async-done(((bf16[16,36,2048]{2,1,0:T(8,128)(2,1)}), bf16[16,36,2048]{2,1,0:T(8,128)(2,1)S(1)}, u32[]{:S(2)}, u32[]{:S(2)}) %all-to-all-start) | async-done | bytes 2359328 | tf_op jit(solution)/shard_map/all_to_all | solution.py:140
  87.6 5.4 all-to-all-start.4
  96.9 56.0 %all-to-all-done.4 = bf16[16,36,2048]{2,1,0:T(8,128)(2,1)} async-done(((bf16[16,36,2048]{2,1,0:T(8,128)(2,1)}), bf16[16,36,2048]{2,1,0:T(8,128)(2,1)}, u32[]{:S(2)}, u32[]{:S(2)}) %all-to-all-start.4) | async-done | bytes 2359328 | tf_op jit(solution)/shard_map/all_to_all | solution.py:267
  163.5 14.8 %all-to-all-done.1 = bf16[4,1,1,384,512]{3,4,2,1,0:T(8,128)(2,1)} async-done(((bf16[4,1,1,384,512]{3,4,2,1,0:T(8,128)(2,1)}), bf16[4,1,1,384,512]{3,4,2,1,0:T(8,128)(2,1)}, u32[]{:S(2)}, u32[]{:S(2)}) %all-to-all-start.1) | async-done | bytes 1572896 | tf_op jit(solution)/shard_map/all_to_all | solution.py:122
  193.2 4.7 reshape.564
  203.3 20.7 %pad_maximum_fusion = bf16[4,589824]{1,0:T(4,128)(2,1)} fusion(bf16[4,196608]{1,0:T(4,128)(2,1)S(1)} %bitcast.166, bf16[4,393216]{1,0:T(4,128)(2,1)} %reshape.564), kind=kLoop, calls=%fused_computation.10 | loop fusion | flops 9437184 | bytes 9437184 | tf_op jit(solution)/shard_map/concatenate | solution.py:46
  224.0 9.2 %reshape.567 = bf16[18432,128]{1,0:T(8,128)(2,1)} reshape(bf16[4,589824]{1,0:T(4,128)(2,1)} %pad_maximum_fusion) | data formatting | bytes 9437184 | tf_op jit(solution)/shard_map/reshape | solution.py:48
  233.3 52.6 %reduce-scatter.2.cloned.1.call-done = bf16[4608,128]{1,0:T(8,128)(2,1)} async-done(((bf16[18432,128]{1,0:T(8,128)(2,1)}), bf16[4608,128]{1,0:T(8,128)(2,1)}) %reduce-scatter.2.cloned.1.call-update) | async-done | bytes 1179664 | tf_op jit(solution)/shard_map/reduce_scatter | solution.py:49
  307.5 7.6 %all-to-all-start.5 = ((bf16[16,2,18432]{2,1,0:T(2,128)(2,1)}), bf16[16,2,18432]{2,1,0:T(2,128)(2,1)S(1)}, u32[]{:S(2)}, u32[]{:S(2)}) async-start(bf16[16,2,18432]{2,1,0:T(2,128)(2,1)} %reshape.678), calls=%async_computation.6 | async-start | bytes 2359296 | tf_op jit(solution)/shard_map/all_to_all | solution.py:23
  323.7 22.1 %all-to-all-done.5 = bf16[16,2,18432]{2,1,0:T(2,128)(2,1)S(1)} async-done(((bf16[16,2,18432]{2,1,0:T(2,128)(2,1)}), bf16[16,2,18432]{2,1,0:T(2,128)(2,1)S(1)}, u32[]{:S(2)}, u32[]{:S(2)}) %all-to-all-start.5) | async-done | bytes 1179680 | tf_op jit(solution)/shard_map/all_to_all | solution.py:23
  346.7 4.8 all-to-all-start.2
  355.5 4.4 reshape.679
  365.2 45.5 %all-to-all-done.2 = bf16[16,36,2048]{2,1,0:T(8,128)(2,1)} async-done(((bf16[16,36,2048]{2,1,0:T(8,128)(2,1)}), bf16[16,36,2048]{2,1,0:T(8,128)(2,1)}, u32[]{:S(2)}, u32[]{:S(2)}) %all-to-all-start.2) | async-done | bytes 2359328 | tf_op jit(solution)/shard_map/all_to_all | solution.py:153
  410.7 5.5 all-to-all-start.7
  419.0 11.7 %all-to-all-done.7 = bf16[16,2,6144]{2,1,0:T(2,128)(2,1)S(1)} async-done(((bf16[16,2,6144]{2,1,0:T(2,128)(2,1)}), bf16[16,2,6144]{2,1,0:T(2,128)(2,1)S(1)}, u32[]{:S(2)}, u32[]{:S(2)}) %all-to-all-start.7) | async-done | bytes 393248 | tf_op jit(solution)/shard_map/all_to_all | solution.py:195
  444.5 12.9 %all-to-all-done.6 = bf16[16,2,12288]{2,1,0:T(2,128)(2,1)} async-done(((bf16[16,2,12288]{2,1,0:T(2,128)(2,1)}), bf16[16,2,12288]{2,1,0:T(2,128)(2,1)}, u32[]{:S(2)}, u32[]{:S(2)}) %all-to-all-start.6) | async-done | bytes 786464 | tf_op jit(solution)/shard_map/all_to_all | solution.py:192
  479.8 13.2 %collective-permute-done = bf16[128,2048]{1,0:T(8,128)(2,1)S(1)} collective-permute-done((bf16[128,2048]{1,0:T(8,128)(2,1)S(1)}, bf16[128,2048]{1,0:T(8,128)(2,1)S(1)}, u32[]{:S(2)}, u32[]{:S(2)}) %collective-permute-start) | collective-permute-done | bytes 524320 | tf_op jit(solution)/shard_map/ppermute | solution.py:60
  503.4 5.6 reduce.6
  516.9 5.8 all-to-all-start.3
  522.7 10.7 %reshape.685 = bf16[16,1,73728]{2,1,0:T(2,128)(2,1)} reshape(bf16[16,2,36864]{2,1,0:T(2,128)(2,1)} %all-to-all-done.10) | data formatting | bytes 4718592
  533.4 4.9 copy.121
  544.5 37.9 %all-to-all-done.3 = bf16[16,36,2048]{2,1,0:T(8,128)(2,1)} async-done(((bf16[16,36,2048]{2,1,0:T(8,128)(2,1)}), bf16[16,36,2048]{2,1,0:T(8,128)(2,1)}, u32[]{:S(2)}, u32[]{:S(2)}) %all-to-all-start.3) | async-done | bytes 2359328 | tf_op jit(solution)/shard_map/all_to_all | solution.py:140
  597.0 11.1 %all-to-all-done.8 = bf16[4,1,1,384,512]{3,4,2,1,0:T(8,128)(2,1)} async-done(((bf16[4,1,1,384,512]{3,4,2,1,0:T(8,128)(2,1)}), bf16[4,1,1,384,512]{3,4,2,1,0:T(8,128)(2,1)}, u32[]{:S(2)}, u32[]{:S(2)}) %all-to-all-start.8) | async-done | bytes 1572896 | tf_op jit(solution)/shard_map/all_to_all | solution.py:122
  608.1 6.8 all-to-all-start.11
  628.7 4.4 fusion.15
  633.2 6.9 convolution_convert_fusion
  644.2 25.0 %all-to-all-done.11 = bf16[16,2,36864]{2,1,0:T(2,128)(2,1)S(1)} async-done(((bf16[16,2,36864]{2,1,0:T(2,128)(2,1)}), bf16[16,2,36864]{2,1,0:T(2,128)(2,1)S(1)}, u32[]{:S(2)}, u32[]{:S(2)}) %all-to-all-start.11) | async-done | bytes 2359328 | tf_op jit(solution)/shard_map/all_to_all | solution.py:23
  670.6 5.5 all-to-all-start.9
  676.2 10.7 %reshape.687 = bf16[16,1,73728]{2,1,0:T(2,128)(2,1)} reshape(bf16[16,2,36864]{2,1,0:T(2,128)(2,1)} %copy-done.2) | data formatting | bytes 4718592
  686.9 4.9 copy.120
  702.2 33.7 %all-to-all-done.9 = bf16[16,36,2048]{2,1,0:T(8,128)(2,1)S(1)} async-done(((bf16[16,36,2048]{2,1,0:T(8,128)(2,1)}), bf16[16,36,2048]{2,1,0:T(8,128)(2,1)S(1)}, u32[]{:S(2)}, u32[]{:S(2)}) %all-to-all-start.9) | async-done | bytes 2359328 | tf_op jit(solution)/shard_map/all_to_all | solution.py:153
  (226 shorter events, 210.7 us)
Async XLA Ops:
  7.2 17.5 %copy-start = (bf16[1,128,2048]{2,1,0:T(8,128)(2,1)S(1)}, bf16[1,128,2048]{2,1,0:T(8,128)(2,1)}, u32[]{:S(2)}) copy-start(bf16[1,128,2048]{2,1,0:T(8,128)(2,1)} %param.19) | copy-start | bytes 1572868
  14.6 10.1 %copy-start.26 = (f32[1,128,2]{1,2,0:T(2,128)S(1)}, f32[1,128,2]{1,2,0:T(2,128)}, u32[]{:S(2)}) copy-start(f32[1,128,2]{1,2,0:T(2,128)} %param.22) | copy-start | bytes 3076
  14.6 69.9 %all-to-all-start = ((bf16[16,36,2048]{2,1,0:T(8,128)(2,1)}), bf16[16,36,2048]{2,1,0:T(8,128)(2,1)S(1)}, u32[]{:S(2)}, u32[]{:S(2)}) async-start(bf16[16,36,2048]{2,1,0:T(8,128)(2,1)} %bitcast.161), calls=%async_computation | async-start | bytes 5242880 | tf_op jit(solution)/shard_map/all_to_all | solution.py:140
  87.6 65.3 %all-to-all-start.4 = ((bf16[16,36,2048]{2,1,0:T(8,128)(2,1)}), bf16[16,36,2048]{2,1,0:T(8,128)(2,1)}, u32[]{:S(2)}, u32[]{:S(2)}) async-start(bf16[16,36,2048]{2,1,0:T(8,128)(2,1)} %bitcast.160), calls=%async_computation.4 | async-start | bytes 5242880 | tf_op jit(solution)/shard_map/all_to_all | solution.py:267
  93.0 89.0 %all-gather.3.cloned.1.call-start = ((), (), s32[]{:S(2)}) async-start(), calls=%async_computation.13 | async-start | bytes 3932160 | tf_op jit(solution)/shard_map/all_gather | solution.py:120
  154.2 24.1 %all-to-all-start.1 = ((bf16[4,1,1,384,512]{3,4,2,1,0:T(8,128)(2,1)}), bf16[4,1,1,384,512]{3,4,2,1,0:T(8,128)(2,1)}, u32[]{:S(2)}, u32[]{:S(2)}) async-start(bf16[4,1,1,384,512]{3,4,2,1,0:T(8,128)(2,1)} %stack.10), calls=%async_computation.1 | async-start | bytes 3145728 | tf_op jit(solution)/shard_map/all_to_all | solution.py:122
  158.5 127.3 %reduce-scatter.2.cloned.1.call-start = ((), (), s32[]{:S(2)}) async-start(), calls=%async_computation.14 | async-start | bytes 5898240 | tf_op jit(solution)/shard_map/reduce_scatter | solution.py:49
  189.0 8.9 %copy-start.21 = (bf16[576,384]{1,0:T(8,128)(2,1)}, bf16[576,384]{1,0:T(8,128)(2,1)S(1)}, u32[]{:S(2)}) copy-start(bf16[576,384]{1,0:T(8,128)(2,1)S(1)} %get-tuple-element.37) | copy-start | bytes 1327108
  294.7 4.7 copy-start.13
  307.5 38.2 %all-to-all-start.5 = ((bf16[16,2,18432]{2,1,0:T(2,128)(2,1)}), bf16[16,2,18432]{2,1,0:T(2,128)(2,1)S(1)}, u32[]{:S(2)}, u32[]{:S(2)}) async-start(bf16[16,2,18432]{2,1,0:T(2,128)(2,1)} %reshape.678), calls=%async_computation.6 | async-start | bytes 2359296 | tf_op jit(solution)/shard_map/all_to_all | solution.py:23
  323.7 27.9 %copy-start.29 = (s32[1,8]{1,0:T(1,128)S(1)}, s32[1,8]{1,0:T(1,128)}, u32[]{:S(2)}) copy-start(s32[1,8]{1,0:T(1,128)} %param.25) | copy-start | bytes 100
  346.7 63.9 %all-to-all-start.2 = ((bf16[16,36,2048]{2,1,0:T(8,128)(2,1)}), bf16[16,36,2048]{2,1,0:T(8,128)(2,1)}, u32[]{:S(2)}, u32[]{:S(2)}) async-start(bf16[16,36,2048]{2,1,0:T(8,128)(2,1)} %reshape.552), calls=%async_computation.2 | async-start | bytes 5242880 | tf_op jit(solution)/shard_map/all_to_all | solution.py:153
  410.7 20.0 %all-to-all-start.7 = ((bf16[16,2,6144]{2,1,0:T(2,128)(2,1)}), bf16[16,2,6144]{2,1,0:T(2,128)(2,1)S(1)}, u32[]{:S(2)}, u32[]{:S(2)}) async-start(bf16[16,2,6144]{2,1,0:T(2,128)(2,1)} %reshape.680), calls=%async_computation.8 | async-start | bytes 786432 | tf_op jit(solution)/shard_map/all_to_all | solution.py:195
  416.4 19.3 %copy-start.15 = (bf16[16,12288]{1,0:T(8,128)(2,1)S(1)}, bf16[16,12288]{1,0:T(8,128)(2,1)}, u32[]{:S(2)}) copy-start(bf16[16,12288]{1,0:T(8,128)(2,1)} %reshape.576) | copy-start | bytes 1179652
  431.4 25.9 %all-to-all-start.6 = ((bf16[16,2,12288]{2,1,0:T(2,128)(2,1)}), bf16[16,2,12288]{2,1,0:T(2,128)(2,1)}, u32[]{:S(2)}, u32[]{:S(2)}) async-start(bf16[16,2,12288]{2,1,0:T(2,128)(2,1)} %reshape.682), calls=%async_computation.7 | async-start | bytes 1572864 | tf_op jit(solution)/shard_map/all_to_all | solution.py:192
  444.5 17.5 %copy-start.27 = (s32[1,128,2]{1,2,0:T(2,128)S(1)}, s32[1,128,2]{1,2,0:T(2,128)}, u32[]{:S(2)}) copy-start(s32[1,128,2]{1,2,0:T(2,128)} %param.23) | copy-start | bytes 3076
  457.4 57.7 %all-to-all-start.10 = ((bf16[16,2,36864]{2,1,0:T(2,128)(2,1)}), bf16[16,2,36864]{2,1,0:T(2,128)(2,1)}, u32[]{:S(2)}, u32[]{:S(2)}) async-start(bf16[16,2,36864]{2,1,0:T(2,128)(2,1)} %reshape.684), calls=%async_computation.11 | async-start | bytes 4718592 | tf_op jit(solution)/shard_map/all_to_all | solution.py:23
  461.7 167.0 %all-gather.5.cloned.1.call-start = ((), (), s32[]{:S(2)}) async-start(), calls=%async_computation.15 | async-start | bytes 3932160 | tf_op jit(solution)/shard_map/all_gather | solution.py:120
  474.8 4.6 slice-start
  474.8 18.4 %copy-start.24 = (f32[1,2048]{1,0:T(1,128)S(1)}, f32[1,2048]{1,0:T(1,128)}, u32[]{:S(2)}) copy-start(f32[1,2048]{1,0:T(1,128)} %param.20) | copy-start | bytes 24580
  478.1 14.9 %collective-permute-start = (bf16[128,2048]{1,0:T(8,128)(2,1)S(1)}, bf16[128,2048]{1,0:T(8,128)(2,1)S(1)}, u32[]{:S(2)}, u32[]{:S(2)}) collective-permute-start(bf16[128,2048]{1,0:T(8,128)(2,1)S(1)} %fusion.34), channel_id=1, source_target_pairs={{192,0},{0,64},{64,128},{128,192},{193,1},{1,65},{65,129},{129,193... | collective-permute-start | bytes 1572872 | tf_op jit(solution)/shard_map/ppermute | solution.py:60
  479.8 15.4 %copy-start.18 = (bf16[16,2,6144]{2,1,0:T(2,128)(2,1)S(1)}, bf16[16,2,6144]{2,1,0:T(2,128)(2,1)}, u32[]{:S(2)}) copy-start(bf16[16,2,6144]{2,1,0:T(2,128)(2,1)} %copy-done.17) | copy-start | bytes 1179652
  495.6 7.8 %copy-start.4 = (bf16[16,1,12288]{2,1,0:T(2,128)(2,1)}, bf16[16,1,12288]{2,1,0:T(2,128)(2,1)S(1)}, u32[]{:S(2)}) copy-start(bf16[16,1,12288]{2,1,0:T(2,128)(2,1)S(1)} %reshape.681) | copy-start | bytes 1179652
  509.1 6.0 copy-start.6
  516.9 65.6 %all-to-all-start.3 = ((bf16[16,36,2048]{2,1,0:T(8,128)(2,1)}), bf16[16,36,2048]{2,1,0:T(8,128)(2,1)}, u32[]{:S(2)}, u32[]{:S(2)}) async-start(bf16[16,36,2048]{2,1,0:T(8,128)(2,1)} %bitcast.18), calls=%async_computation.3 | async-start | bytes 5242880 | tf_op jit(solution)/shard_map/all_to_all | solution.py:140
  542.3 40.2 %copy-start.19 = (bf16[384,512]{0,1:T(8,128)(2,1)S(1)}, bf16[384,512]{0,1:T(8,128)(2,1)}, u32[]{:S(2)}) copy-start(bf16[384,512]{0,1:T(8,128)(2,1)} %copy.93) | copy-start | bytes 1179652
  544.5 43.6 %copy-start.16 = (bf16[16,12288]{1,0:T(8,128)(2,1)S(1)}, bf16[16,12288]{1,0:T(8,128)(2,1)}, u32[]{:S(2)}) copy-start(bf16[16,12288]{1,0:T(8,128)(2,1)} %get-tuple-element.36) | copy-start | bytes 1179652
  583.7 24.3 %all-to-all-start.8 = ((bf16[4,1,1,384,512]{3,4,2,1,0:T(8,128)(2,1)}), bf16[4,1,1,384,512]{3,4,2,1,0:T(8,128)(2,1)}, u32[]{:S(2)}, u32[]{:S(2)}) async-start(bf16[4,1,1,384,512]{3,4,2,1,0:T(8,128)(2,1)} %stack.27), calls=%async_computation.9 | async-start | bytes 3145728 | tf_op jit(solution)/shard_map/all_to_all | solution.py:122
  597.0 18.2 %copy-start.28 = (f32[1,128,2]{1,2,0:T(2,128)S(1)}, f32[1,128,2]{1,2,0:T(2,128)}, u32[]{:S(2)}) copy-start(f32[1,128,2]{1,2,0:T(2,128)} %param.24) | copy-start | bytes 3076
  608.1 61.1 %all-to-all-start.11 = ((bf16[16,2,36864]{2,1,0:T(2,128)(2,1)}), bf16[16,2,36864]{2,1,0:T(2,128)(2,1)S(1)}, u32[]{:S(2)}, u32[]{:S(2)}) async-start(bf16[16,2,36864]{2,1,0:T(2,128)(2,1)} %reshape.686), calls=%async_computation.12 | async-start | bytes 4718592 | tf_op jit(solution)/shard_map/all_to_all | solution.py:23
  670.6 65.2 %all-to-all-start.9 = ((bf16[16,36,2048]{2,1,0:T(8,128)(2,1)}), bf16[16,36,2048]{2,1,0:T(8,128)(2,1)S(1)}, u32[]{:S(2)}, u32[]{:S(2)}) async-start(bf16[16,36,2048]{2,1,0:T(8,128)(2,1)} %reshape.569), calls=%async_computation.10 | async-start | bytes 5242880 | tf_op jit(solution)/shard_map/all_to_all | solution.py:153
  742.5 6.7 copy-start.1
  (17 other events, 42.8 us)
Sparse Core Ops, SparseCore 0:
  96.2 43.1 all-gather.2
  233.4 52.4 reduce-scatter.1
  511.7 39.5 all-gather.4
